TPU v7x, 32 devices: a whole 2x2x4 slice. The times are simulated.
32 devices in a mesh: dp: 4 (over y, x), ctx: 8 (over z, core).
Axes of the slice: x: 2, y: 2, z: 4, core: 2. Of those that a mesh axis runs over, the one named last changes fastest.
Arguments:
- hidden: bfloat16 [4, 4096, 8192], P('dp', 'ctx'), may hold values from -8 to 8
- norm_gain: float32 [8192], replicated, may hold values from 0.3 to 5.2
- cotangent: bfloat16 [4, 4096, 512], P('dp', 'ctx'), may hold values from -30 to 30
- loss_weight: float32 [4], P('dp'), may hold values from 0.08 to 5
Outputs:
- clipped_grad: float32 [8192, 512], P('ctx', 'dp')
All inputs are finite; a program needn't handle non-finite values.
Results may differ from a plain program's by a relative error of at most 0.0022.
Values may be sent and summed in bfloat16 or wider, within the bound.
A program may use at most 64 MiB of HBM per device.

v0:
```python
import math

import jax
import jax.numpy as jnp
from jax import lax
from jax.sharding import PartitionSpec as P


def per_device(hidden, norm_gain, cotangent, loss_weight):
    widened = hidden[0].astype(jnp.float32)
    scale = lax.rsqrt(jnp.mean(widened * widened, axis=1, keepdims=True) + 1e-05)
    normed = (widened * scale * norm_gain).astype(jnp.bfloat16)
    upstream = cotangent[0]
    context_size = lax.axis_size("ctx")
    doc_length = upstream.shape[0] * context_size
    weight = loss_weight[0] / math.sqrt(doc_length)
    features = normed.shape[1]
    outputs = upstream.shape[1]
    contract = (((0,), (0,)), ((), ()))
    owned_tile = lax.psum_scatter(
        weight * lax.dot_general(normed, upstream, contract, preferred_element_type=jnp.float32),
        "ctx",
        scatter_dimension=0,
        tiled=True,
    )
    squares = jnp.sum(owned_tile * owned_tile)
    clip_bound = math.sqrt(features * outputs)
    summed = lax.psum(squares, "ctx")
    factor = jnp.minimum(1.0, clip_bound * lax.rsqrt(summed + 1e-06))
    result = lax.psum_scatter(factor * owned_tile, "dp", scatter_dimension=1, tiled=True)
    return result


def solution(mesh):
    in_specs = (P("dp", "ctx", None), P(), P("dp", "ctx", None), P("dp"))
    out_specs = P("ctx", "dp")
    return jax.shard_map(
        per_device, mesh=mesh, in_specs=in_specs, out_specs=out_specs, check_vma=False
    )
```

profile of v0, /device:TPU:0, one launch (start us, length us, event | category | flops | bytes accessed | tf_op | source)
XLA Modules:
  0.0 254.4 jit_solution(13900599546255570050)
XLA Ops:
  6.5 0.0 copy-start
  6.5 0.0 reduce-scatter.3.cloned.1.call-start
  6.5 0.0 copy-start.1
  7.3 5.5 %fusion = f32[512]{0:T(512)S(1)} fusion(bf16[1,512,8192]{2,1,0:T(8,128)(2,1)} %param.4), kind=kLoop, calls=%fused_computation.2 | loop fusion | flops 12582400 | bytes 8390656 | tf_op jit(solution)/shard_map/reduce_sum | solution.py:11
  12.8 0.0 copy-done
  12.8 0.0 copy-done.1
  12.8 9.1 %convolution_multiply_fusion = f32[8192,512]{1,0:T(8,128)} fusion(bf16[1,512,8192]{2,1,0:T(8,128)(2,1)S(1)} %copy-done.1, f32[8192]{0:T(1024)} %param.5, f32[512]{0:T(512)S(1)} %add_rsqrt_fusion, f32[]{:T(128)} %bitcast, bf16[1,512,512]{2,1,0:T(8,128)(2,1)S(1)} %copy-done), kind=kOutput, calls=%fused_computation.5 | convolution fusion | flops 4315938816 | bytes 25724932 | tf_op jit(solution)/shard_map/dot_general | solution.py:21
  21.9 0.0 reduce-scatter.3.cloned.1.call-update
  22.0 0.0 reduce-scatter.5.cloned.1.call-start
  22.0 171.0 %reduce-scatter.3.cloned.1.call-done = f32[1024,512]{1,0:T(8,128)} async-done(((f32[8192,512]{1,0:T(8,128)}), f32[1024,512]{1,0:T(8,128)}) %reduce-scatter.3.cloned.1.call-update) | async-done | bytes 2097168 | tf_op jit(solution)/shard_map/reduce_scatter | solution.py:20
  193.0 2.7 %multiply_reduce_fusion = f32[]{:T(128)} fusion(f32[1024,512]{1,0:T(8,128)} %reduce-scatter.3.cloned.1.call-done), kind=kLoop, calls=%fused_computation.9 | loop fusion | flops 1048575 | bytes 2097156 | tf_op jit(solution)/shard_map/reduce_sum | solution.py:26
  195.7 14.3 %psum.7 = f32[]{:T(128)} all-reduce(f32[]{:T(128)} %multiply_reduce_fusion), channel_id=1, replica_groups=mesh['dp'=4,'ctx'=8] {'ctx'}, use_global_device_ids=true, to_apply=%region_3.0 | all-reduce | flops 1 | bytes 8 | tf_op jit(solution)/shard_map/psum | solution.py:28
  210.7 3.2 %broadcast_multiply_fusion = f32[1024,512]{1,0:T(8,128)} fusion(f32[1024,512]{1,0:T(8,128)} %reduce-scatter.3.cloned.1.call-done, f32[]{:T(128)S(6)} %min_shard_map.3), kind=kLoop, calls=%fused_computation.10 | loop fusion | flops 524288 | bytes 4194308 | tf_op jit(solution)/shard_map/mul | solution.py:30
  213.9 0.0 reduce-scatter.5.cloned.1.call-update
  213.9 33.7 %reduce-scatter.5.cloned.1.call-done = f32[1024,128]{1,0:T(8,128)} async-done(((f32[1024,512]{1,0:T(8,128)}), f32[1024,128]{1,0:T(8,128)}) %reduce-scatter.5.cloned.1.call-update) | async-done | bytes 524304 | tf_op jit(solution)/shard_map/reduce_scatter | solution.py:30
  (1 shorter events, 0.0 us)
Async XLA Ops:
  6.5 6.3 %copy-start = (bf16[1,512,512]{2,1,0:T(8,128)(2,1)S(1)}, bf16[1,512,512]{2,1,0:T(8,128)(2,1)}, u32[]{:S(2)}) copy-start(bf16[1,512,512]{2,1,0:T(8,128)(2,1)} %param.6) | copy-start | bytes 1572868
  6.5 186.4 %reduce-scatter.3.cloned.1.call-start = ((), (), s32[]{:S(2)}) async-start(), calls=%async_computation.2 | async-start | bytes 18874368 | tf_op jit(solution)/shard_map/reduce_scatter | solution.py:20
  6.5 6.3 %copy-start.1 = (bf16[1,512,8192]{2,1,0:T(8,128)(2,1)S(1)}, bf16[1,512,8192]{2,1,0:T(8,128)(2,1)}, u32[]{:S(2)}) copy-start(bf16[1,512,8192]{2,1,0:T(8,128)(2,1)} %param.4) | copy-start | bytes 25165828
  22.0 225.6 %reduce-scatter.5.cloned.1.call-start = ((), (), s32[]{:S(2)}) async-start(), calls=%async_computation.3 | async-start | bytes 2621440 | tf_op jit(solution)/shard_map/reduce_scatter | solution.py:30
Sparse Core Ops, SparseCore 0:
  22.1 170.8 reduce-scatter.2
  214.0 33.4 reduce-scatter.4
where the time goes:
time: 255 us; the launch traced here: 254 us
  waiting for transfers between devices  205 us (80%)
  between operations  14.9 us (6%)
  blocking collectives  14.3 us (6%)
  other arithmetic  11.4 us (4%)
  matrix products  9.1 us (4%)
    reduce_scatter x1, waiting for transfers between devices, per_device(): lax.psum_scatter(weight * lax.dot_general(normed, upstream, contract, pre...  171 us
    reduce_scatter x1, waiting for transfers between devices, per_device(): lax.psum_scatter(factor * owned_tile, 'dp', scatter_dimension=1, tiled=True)  33.7 us
    psum x1, blocking collectives, per_device(): summed = lax.psum(squares, 'ctx')  14.3 us
    dot_general x1, matrix products, per_device(): lax.dot_general(normed, upstream, contract, preferred_element_type=jnp.fl...  9.1 us
    reduce_sum x1, other arithmetic, per_device(): jnp.mean(widened * widened, axis=1, keepdims=True) + 1e-05  5.46 us
  transfers between devices with their start and end apart: 2, of which 2 were waited for; matrix products, arithmetic and copies ran while one was open for 0% of the time, Pallas kernels for 0%

commit v1 on v0

--- a/solution.py
+++ b/solution.py
@@ -1,9 +1,16 @@
+import functools
 import math
 
 import jax
 import jax.numpy as jnp
 from jax import lax
+from jax.experimental import pallas as pl
+from jax.experimental.pallas import tpu as pltpu
 from jax.sharding import PartitionSpec as P
+
+MESH = pl.DeviceIdType.MESH
+CORES = 2
+LAG = 2
 
 
 def per_device(hidden, norm_gain, cotangent, loss_weight):
@@ -31,9 +38,324 @@
     return result
 
 
+def kernel(
+    cfg,
+    hid_ref,
+    gain_ref,
+    cot_ref,
+    w_ref,
+    out_ref,
+    nm,
+    pn,
+    ct,
+    acc,
+    sbuf,
+    rbuf,
+    fin,
+    dpbuf,
+    sqacc,
+    sqbuf,
+    relsend,
+    relrecv,
+    xs,
+    xr,
+    cs,
+    cr,
+    zs,
+    zr,
+    ds_,
+    dr,
+    ss,
+    sr,
+    rs,
+    rr,
+):
+    (tokens, features, outs, line, ndp, oc, fc, rows, inv_len, bound) = cfg
+    block = features // (CORES * line)
+    half = features // CORES // 2
+    ftiles = half // fc
+    ohalves = outs // oc
+    chunks = ftiles * ohalves
+    owned = outs // ndp
+    per_half = oc // owned
+    dp = lax.axis_index("dp")
+    ctx = lax.axis_index("ctx")
+    q = ctx // CORES
+    k = ctx % CORES
+    other = ctx - k + (1 - k)
+    side = q // (line - 1)
+    is_end = (q == 0) | (q == line - 1)
+    down = ctx - CORES
+    up = ctx + CORES
+
+    ends = []
+    for a in range(ndp):
+        for b in range(2):
+            for c in range(CORES):
+                if a + b + c > 0:
+                    pos = ((side + b) % 2) * (line - 1) * CORES + (k + c) % CORES
+                    ends.append(((a * 2 + b) * CORES + c, ((dp + a) % ndp, pos)))
+
+    bar = pltpu.get_barrier_semaphore()
+    pl.semaphore_signal(bar, inc=1, device_id=(dp, other), device_id_type=MESH)
+
+    @pl.when(q > 0)
+    def _():
+        pl.semaphore_signal(bar, inc=1, device_id=(dp, down), device_id_type=MESH)
+
+    @pl.when(q < line - 1)
+    def _():
+        pl.semaphore_signal(bar, inc=1, device_id=(dp, up), device_id_type=MESH)
+
+    @pl.when(is_end)
+    def _():
+        for slot, peer in ends:
+            if slot != 1:
+                pl.semaphore_signal(bar, inc=1, device_id=peer, device_id_type=MESH)
+        pl.semaphore_wait(bar, len(ends) + 1)
+
+    @pl.when(jnp.logical_not(is_end))
+    def _():
+        pl.semaphore_wait(bar, 3)
+
+    ct[0] = cot_ref[...].T
+    cot_copy = pltpu.make_async_remote_copy(
+        src_ref=ct.at[0], dst_ref=ct.at[1], send_sem=cs, recv_sem=cr,
+        device_id=(dp, other), device_id_type=MESH,
+    )
+    cot_copy.start()
+
+    groups = xs.shape[0]
+    grows = tokens // groups
+
+    def norm_copy(g):
+        at = pl.ds(pl.multiple_of(g * grows, grows), grows)
+        return pltpu.make_async_remote_copy(
+            src_ref=nm.at[1 - k, at], dst_ref=pn.at[at], send_sem=xs.at[g], recv_sem=xr.at[g],
+            device_id=(dp, other), device_id_type=MESH,
+        )
+
+    def norm_rows(i, carry):
+        at = pl.ds(pl.multiple_of(i * rows, rows), rows)
+        total = jnp.zeros((rows, block), jnp.float32)
+        for j in range(CORES * line):
+            v = hid_ref[at, j * block : (j + 1) * block].astype(jnp.float32)
+            total = total + v * v
+        mean = jnp.sum(total, axis=1, keepdims=True) * (1.0 / features)
+        scale = lax.rsqrt(mean + 1e-05)
+        for j in range(CORES * line):
+            v = hid_ref[at, j * block : (j + 1) * block].astype(jnp.float32)
+            g = gain_ref[:, j * block : (j + 1) * block]
+            local = (j // CORES) * block
+            nm[j % CORES, at, local : local + block] = (v * scale * g).astype(jnp.bfloat16)
+        return carry
+
+    def norm_group(g, carry):
+        per = grows // rows
+        lax.fori_loop(g * per, (g + 1) * per, norm_rows, 0)
+        norm_copy(g).start()
+        return carry
+
+    lax.fori_loop(0, groups, norm_group, 0)
+    sqacc[...] = jnp.zeros_like(sqacc)
+    cot_copy.wait()
+    lax.fori_loop(0, groups, lambda g, c: (norm_copy(g).wait(), c)[1], 0)
+
+    def z_copy(d, s):
+        return pltpu.make_async_remote_copy(
+            src_ref=sbuf.at[d, s], dst_ref=rbuf.at[d, s], send_sem=zs.at[d, s],
+            recv_sem=zr.at[d, s], device_id=(dp, down if d == 0 else up), device_id_type=MESH,
+        )
+
+    def dp_copy(a, ft):
+        d = (dp + a) % ndp
+        return pltpu.make_async_remote_copy(
+            src_ref=fin.at[pl.ds(pl.multiple_of(d * owned, owned), owned),
+                           pl.ds(pl.multiple_of(ft * fc, fc), fc)],
+            dst_ref=dpbuf.at[a - 1, :, pl.ds(pl.multiple_of(ft * fc, fc), fc)],
+            send_sem=ds_.at[a - 1, ft], recv_sem=dr.at[a - 1, ft],
+            device_id=(d, ctx), device_id_type=MESH,
+        )
+
+    def process(d, s):
+        ft = s // ohalves
+        h = s % ohalves
+        local = pl.ds(pl.multiple_of(d * half + ft * fc, fc), fc)
+        orow = pl.ds(pl.multiple_of(h * oc, oc), oc)
+        first = q == (line - 1 if d == 0 else 0)
+        last = q == (0 if d == 0 else line - 1)
+        acc[d] = jnp.dot(
+            ct[0, orow, :], nm[k, :, local], preferred_element_type=jnp.float32
+        ) + jnp.dot(ct[1, orow, :], pn[:, local], preferred_element_type=jnp.float32)
+
+        @pl.when(first)
+        def _():
+            sbuf[d, s] = acc[d].astype(jnp.bfloat16)
+            z_copy(d, s).start()
+
+        @pl.when(jnp.logical_not(first | last))
+        def _():
+            z_copy(d, s).wait_recv()
+            sbuf[d, s] = (acc[d] + rbuf[d, s].astype(jnp.float32)).astype(jnp.bfloat16)
+            z_copy(d, s).start()
+
+        @pl.when(last)
+        def _():
+            z_copy(d, s).wait_recv()
+            tile = acc[d] + rbuf[d, s].astype(jnp.float32)
+            fin[orow, pl.ds(pl.multiple_of(ft * fc, fc), fc)] = tile
+            sqacc[...] += jnp.sum((tile * tile).reshape(oc // 8, 8, fc), axis=0)
+            for a in range(1, ndp):
+
+                @pl.when(((dp + a) % ndp) // per_half == h)
+                def _():
+                    dp_copy(a, ft).start()
+
+    def step(t, carry):
+        for d in range(2):
+            s = t - ((line - 1 - q) if d == 0 else q) * LAG
+
+            @pl.when((s >= 0) & (s < chunks))
+            def _():
+                process(d, s)
+
+        return carry
+
+    lax.fori_loop(0, chunks + (line - 1) * LAG, step, 0)
+
+    def z_done(s, carry):
+        @pl.when(q > 0)
+        def _():
+            z_copy(0, s).wait_send()
+
+        @pl.when(q < line - 1)
+        def _():
+            z_copy(1, s).wait_send()
+
+        return carry
+
+    def rel_copy(i, to):
+        at = pl.ds(i * fc, fc)
+        return pltpu.make_async_remote_copy(
+            src_ref=relsend.at[at], dst_ref=relrecv.at[at], send_sem=rs.at[i], recv_sem=rr.at[i],
+            device_id=(dp, to), device_id_type=MESH,
+        )
+
+    rtiles = block // fc
+
+    def ending(sd):
+        toward = up if sd == 0 else down
+        weight = w_ref[0, 0] * inv_len
+        sq = jnp.sum(jnp.sum(sqacc[...], axis=1, keepdims=True), axis=0, keepdims=True)
+        row = lax.broadcasted_iota(jnp.int32, (8, 128), 0)
+        sqbuf[0] = jnp.where(row == 0, jnp.broadcast_to(sq * (weight * weight), (8, 128)), weight)
+        sends = [
+            pltpu.make_async_remote_copy(
+                src_ref=sqbuf.at[0], dst_ref=sqbuf.at[slot], send_sem=ss.at[slot - 1],
+                recv_sem=sr.at[slot - 1], device_id=peer, device_id_type=MESH,
+            )
+            for slot, peer in ends
+        ]
+        for c in sends:
+            c.start()
+        for a in range(1, ndp):
+            lax.fori_loop(0, ftiles, lambda ft, c, a=a: (dp_copy(a, ft).wait(), c)[1], 0)
+        for c in sends:
+            c.wait()
+        mult = []
+        for a in range(ndp):
+            base = a * 2 * CORES
+            total = sqbuf[base, 0:1, :]
+            for i in range(1, 2 * CORES):
+                total = total + sqbuf[base + i, 0:1, :]
+            factor = jnp.minimum(1.0, bound * lax.rsqrt(total + 1e-06))
+            mult.append((factor * sqbuf[base, 1:2, :])[:, 0:1])
+        mine = pl.ds(pl.multiple_of(dp * owned, owned), owned)
+
+        def combine(f0):
+            cols = slice(f0, f0 + fc)
+            value = fin[mine, cols] * mult[0]
+            for a in range(1, ndp):
+                value = value + dpbuf[a - 1, :, cols] * mult[a]
+            return value.T
+
+        far, near = (block, 0) if sd == 0 else (0, block)
+        for i in range(rtiles):
+            relsend[i * fc : (i + 1) * fc, :] = combine(far + i * fc)
+            rel_copy(i, toward).start()
+        for i in range(rtiles):
+            out_ref[i * fc : (i + 1) * fc, :] = combine(near + i * fc)
+        lax.fori_loop(0, chunks, z_done, 0)
+        for i in range(rtiles):
+            rel_copy(i, toward).wait_send()
+
+    @pl.when(q == 0)
+    def _():
+        ending(0)
+
+    @pl.when(q == line - 1)
+    def _():
+        ending(1)
+
+    @pl.when(jnp.logical_not(is_end))
+    def _():
+        lax.fori_loop(0, chunks, z_done, 0)
+        for i in range(rtiles):
+            rel_copy(i, down).wait_recv()
+            out_ref[i * fc : (i + 1) * fc, :] = relrecv[i * fc : (i + 1) * fc, :]
+
+
+def fused(hidden, norm_gain, cotangent, loss_weight):
+    _, tokens, features = hidden.shape
+    outs = cotangent.shape[2]
+    ctx = lax.axis_size("ctx")
+    ndp = lax.axis_size("dp")
+    line = ctx // CORES
+    block = features // ctx
+    half = features // CORES // 2
+    owned = outs // ndp
+    oc, fc, rows, groups = outs // 2, 256, 16, 4
+    ftiles = half // fc
+    chunks = ftiles * (outs // oc)
+    cfg = (tokens, features, outs, line, ndp, oc, fc, rows,
+           1.0 / math.sqrt(tokens * ctx), math.sqrt(features * outs))
+    bf16, f32 = jnp.bfloat16, jnp.float32
+    dma = pltpu.SemaphoreType.DMA
+    vmem = pl.BlockSpec(memory_space=pltpu.VMEM)
+    return pl.pallas_call(
+        functools.partial(kernel, cfg),
+        name="clipped_grad",
+        out_shape=jax.ShapeDtypeStruct((block, owned), f32),
+        in_specs=[vmem, vmem, vmem, pl.BlockSpec(memory_space=pltpu.SMEM)],
+        out_specs=vmem,
+        scratch_shapes=[
+            pltpu.VMEM((CORES, tokens, features // CORES), bf16),
+            pltpu.VMEM((tokens, features // CORES), bf16),
+            pltpu.VMEM((CORES, outs, tokens), bf16),
+            pltpu.VMEM((2, oc, fc), f32),
+            pltpu.VMEM((2, chunks, oc, fc), bf16),
+            pltpu.VMEM((2, chunks, oc, fc), bf16),
+            pltpu.VMEM((outs, half), f32),
+            pltpu.VMEM((ndp - 1, owned, half), f32),
+            pltpu.VMEM((8, fc), f32),
+            pltpu.VMEM((ndp * 2 * CORES, 8, 128), f32),
+            pltpu.VMEM((block, owned), f32),
+            pltpu.VMEM((block, owned), f32),
+            dma((groups,)), dma((groups,)),
+            dma(()), dma(()),
+            dma((2, chunks)), dma((2, chunks)),
+            dma((ndp - 1, ftiles)), dma((ndp - 1, ftiles)),
+            dma((ndp * 2 * CORES - 1,)), dma((ndp * 2 * CORES - 1,)),
+            dma((block // fc,)), dma((block // fc,)),
+        ],
+        compiler_params=pltpu.CompilerParams(
+            collective_id=0, has_side_effects=True, vmem_limit_bytes=60 << 20
+        ),
+    )(hidden[0], norm_gain[None, :], cotangent[0], loss_weight[None, :])
+
+
 def solution(mesh):
     in_specs = (P("dp", "ctx", None), P(), P("dp", "ctx", None), P("dp"))
     out_specs = P("ctx", "dp")
-    return jax.shard_map(
-        per_device, mesh=mesh, in_specs=in_specs, out_specs=out_specs, check_vma=False
-    )
+    body = fused if mesh.shape["ctx"] == 4 * CORES else per_device
+    return jax.shard_map(body, mesh=mesh, in_specs=in_specs, out_specs=out_specs, check_vma=False)

time: 255 us -> 98.2 us (0.39)
  the two profiles are of different devices: /device:TPU:0 before, /device:TPU:20 now
where the time goes in v1:
time: 98.2 us; the launch traced here: 98.1 us
  Pallas kernels  95.5 us (97%)
  local copies, waits for them, and re-layouts  1.87 us (2%)
    pallas_call x1, Pallas kernels, fused(): pl.pallas_call(functools.partial(kernel, cfg), name='clipped_grad', out_s...  95.5 us

profile of v1, /device:TPU:20, one launch (start us, length us, event | category | flops | bytes accessed | tf_op | source)
XLA Modules:
  0.0 98.1 jit_solution(608214739055477156)
XLA Ops:
  0.7 95.5 %clipped_grad.1 = f32[1024,128]{1,0:T(8,128)} custom-call(bf16[512,8192]{1,0:T(8,128)(2,1)} %bitcast.5, f32[1,8192]{1,0:T(1,128)} %bitcast.7, bf16[512,512]{1,0:T(8,128)(2,1)} %bitcast.6, f32[1,1]{1,0:T(1,128)} %bitcast.4.w_ref), custom_call_target="tpu_custom_call" | custom-call | tf_op jit(solution)/shard_map/clipped_grad/pallas_call | solution.py:325
  96.2 1.9 %copy.7 = f32[1024,128]{1,0:T(8,128)} copy(f32[1024,128]{1,0:T(8,128)} %clipped_grad.1) | data formatting | bytes 1048576

commit v2 on v1

v2 whole, which is shorter than its diff:
```python
import functools
import math

import jax
import jax.numpy as jnp
from jax import lax
from jax.experimental import pallas as pl
from jax.experimental.pallas import tpu as pltpu
from jax.sharding import PartitionSpec as P

MESH = pl.DeviceIdType.MESH
CORES = 2
LAG = 4


def per_device(hidden, norm_gain, cotangent, loss_weight):
    widened = hidden[0].astype(jnp.float32)
    scale = lax.rsqrt(jnp.mean(widened * widened, axis=1, keepdims=True) + 1e-05)
    normed = (widened * scale * norm_gain).astype(jnp.bfloat16)
    upstream = cotangent[0]
    context_size = lax.axis_size("ctx")
    doc_length = upstream.shape[0] * context_size
    weight = loss_weight[0] / math.sqrt(doc_length)
    features = normed.shape[1]
    outputs = upstream.shape[1]
    contract = (((0,), (0,)), ((), ()))
    owned_tile = lax.psum_scatter(
        weight * lax.dot_general(normed, upstream, contract, preferred_element_type=jnp.float32),
        "ctx",
        scatter_dimension=0,
        tiled=True,
    )
    squares = jnp.sum(owned_tile * owned_tile)
    clip_bound = math.sqrt(features * outputs)
    summed = lax.psum(squares, "ctx")
    factor = jnp.minimum(1.0, clip_bound * lax.rsqrt(summed + 1e-06))
    result = lax.psum_scatter(factor * owned_tile, "dp", scatter_dimension=1, tiled=True)
    return result


def flip(v, m):
    return ((v // 2 + m // 2) % 2) * 2 + (v % 2 + m % 2) % 2


def kernel(
    cfg,
    hid_ref,
    gain_ref,
    cot_ref,
    w_ref,
    out_ref,
    hv,
    pr,
    ct,
    sc,
    nt,
    acc,
    sbuf,
    rbuf,
    fin,
    dpbuf,
    sqacc,
    sqbuf,
    relsend,
    relrecv,
    ls,
    xs,
    xr,
    es,
    er,
    zs,
    zr,
    ds_,
    dr,
    ss,
    sr,
    rs,
    rr,
):
    (tokens, features, outs, line, ndp, fc, rows, inv_len, bound) = cfg
    block = features // (CORES * line)
    half = features // CORES // 2
    ftiles = half // fc
    owned = outs // ndp
    chunks = ftiles * ndp
    groups = ls.shape[0]
    grows = tokens // groups
    pieces = xs.shape[0] // 2
    pw = half // pieces
    dp = lax.axis_index("dp")
    ctx = lax.axis_index("ctx")
    q = ctx // CORES
    k = ctx % CORES
    other = ctx - k + (1 - k)
    side = q // (line - 1)
    is_end = (q == 0) | (q == line - 1)
    down = ctx - CORES
    up = ctx + CORES

    ends = []
    for a in range(ndp):
        for b in range(2):
            for c in range(CORES):
                if a + b + c > 0:
                    pos = ((side + b) % 2) * (line - 1) * CORES + (k + c) % CORES
                    ends.append(((a * 2 + b) * CORES + c, (flip(dp, a), pos)))

    bar = pltpu.get_barrier_semaphore()
    pl.semaphore_signal(bar, inc=1, device_id=(dp, other), device_id_type=MESH)

    @pl.when(q > 0)
    def _():
        pl.semaphore_signal(bar, inc=1, device_id=(dp, down), device_id_type=MESH)

    @pl.when(q < line - 1)
    def _():
        pl.semaphore_signal(bar, inc=1, device_id=(dp, up), device_id_type=MESH)

    @pl.when(is_end)
    def _():
        for slot, peer in ends:
            if slot != 1:
                pl.semaphore_signal(bar, inc=1, device_id=peer, device_id_type=MESH)

    def load(g):
        at = pl.ds(pl.multiple_of(g * grows, grows), grows)
        return pltpu.make_async_copy(hid_ref.at[at], hv.at[at], ls.at[g])

    for g in range(groups):
        load(g).start()
    ct[0] = cot_ref[...].T

    @pl.when(is_end)
    def _():
        pl.semaphore_wait(bar, len(ends) + 1)

    @pl.when(jnp.logical_not(is_end))
    def _():
        pl.semaphore_wait(bar, 3)

    def place(d, local, core):
        return (CORES * (d * (line // 2) + local // block) + core) * block + local % block

    def piece_copy(d, p):
        src = pl.ds(pl.multiple_of(place(d, p * pw, 1 - k), pw), pw)
        return pltpu.make_async_remote_copy(
            src_ref=hid_ref.at[:, src], dst_ref=pr.at[:, pl.ds(d * half + p * pw, pw)],
            send_sem=xs.at[2 * p + d], recv_sem=xr.at[2 * p + d],
            device_id=(dp, other), device_id_type=MESH,
        )

    def extra_copy(buf, i):
        return pltpu.make_async_remote_copy(
            src_ref=buf.at[0], dst_ref=buf.at[1], send_sem=es.at[i], recv_sem=er.at[i],
            device_id=(dp, other), device_id_type=MESH,
        )

    for p in range(pieces):
        for d in range(2):
            piece_copy(d, p).start()
        if p == 0:
            extra_copy(ct, 0).start()

    def stat_rows(i, carry):
        at = pl.ds(pl.multiple_of(i * rows, rows), rows)
        total = jnp.zeros((rows, block), jnp.float32)
        for j in range(CORES * line):
            v = hv[at, j * block : (j + 1) * block].astype(jnp.float32)
            total = total + v * v
        mean = jnp.sum(total, axis=1, keepdims=True) * (1.0 / features)
        sc[0, at, :] = jnp.broadcast_to(lax.rsqrt(mean + 1e-05), (rows, 128))
        return carry

    def stat_group(g, carry):
        load(g).wait()
        per = grows // rows
        lax.fori_loop(g * per, (g + 1) * per, stat_rows, 0)
        return carry

    lax.fori_loop(0, groups, stat_group, 0)
    extra_copy(sc, 1).start()
    sqacc[...] = jnp.zeros_like(sqacc)
    extra_copy(ct, 0).wait()
    extra_copy(sc, 1).wait()

    def z_copy(d, s):
        return pltpu.make_async_remote_copy(
            src_ref=sbuf.at[d, s], dst_ref=rbuf.at[d, s], send_sem=zs.at[d, s],
            recv_sem=zr.at[d, s], device_id=(dp, down if d == 0 else up), device_id_type=MESH,
        )

    def dp_copy(m, ft):
        h = flip(dp, m)
        cols = pl.ds(pl.multiple_of(ft * fc, fc), fc)
        return pltpu.make_async_remote_copy(
            src_ref=fin.at[pl.ds(pl.multiple_of(h * owned, owned), owned), cols],
            dst_ref=dpbuf.at[m - 1, :, cols],
            send_sem=ds_.at[m - 1, ft], recv_sem=dr.at[m - 1, ft],
            device_id=(h, ctx), device_id_type=MESH,
        )

    def multiply(d, ft):
        for p in range(pieces):

            @pl.when(ft * fc == p * pw)
            def _():
                piece_copy(d, p).wait()

        own = pl.multiple_of(place(d, ft * fc, k), fc)
        got = pl.multiple_of(d * half + ft * fc, fc)

        def norm_rows(i, carry):
            at = pl.ds(pl.multiple_of(i * 64, 64), 64)
            low = pl.ds(pl.multiple_of(tokens + i * 64, 64), 64)
            for c in range(0, fc, 128):
                g = gain_ref[:, pl.ds(pl.multiple_of(own + c, 128), 128)]
                v = hv[at, pl.ds(pl.multiple_of(own + c, 128), 128)].astype(jnp.float32)
                nt[d, at, c : c + 128] = (v * sc[0, at, :] * g).astype(jnp.bfloat16)
                v = pr[at, pl.ds(pl.multiple_of(got + c, 128), 128)].astype(jnp.float32)
                nt[d, low, c : c + 128] = (v * sc[1, at, :] * g).astype(jnp.bfloat16)
            return carry

        lax.fori_loop(0, tokens // 64, norm_rows, 0)
        acc[d] = jnp.dot(
            ct[0], nt[d, :tokens, :], preferred_element_type=jnp.float32
        ) + jnp.dot(ct[1], nt[d, tokens:, :], preferred_element_type=jnp.float32)

    def process(d, s):
        ft = s // ndp
        m = ndp - 1 - s % ndp
        h = flip(dp, m)
        orow = pl.ds(pl.multiple_of(h * owned, owned), owned)
        first = q == (line - 1 if d == 0 else 0)
        last = q == (0 if d == 0 else line - 1)

        @pl.when(m == ndp - 1)
        def _():
            multiply(d, ft)

        @pl.when(first)
        def _():
            sbuf[d, s] = acc[d, orow, :].astype(jnp.bfloat16)
            z_copy(d, s).start()

        @pl.when(jnp.logical_not(first | last))
        def _():
            z_copy(d, s).wait_recv()
            sbuf[d, s] = (acc[d, orow, :] + rbuf[d, s].astype(jnp.float32)).astype(jnp.bfloat16)
            z_copy(d, s).start()

        @pl.when(last)
        def _():
            z_copy(d, s).wait_recv()
            tile = acc[d, orow, :] + rbuf[d, s].astype(jnp.float32)
            fin[orow, pl.ds(pl.multiple_of(ft * fc, fc), fc)] = tile
            sqacc[...] += jnp.sum((tile * tile).reshape(owned // 8, 8, fc), axis=0)

            @pl.when(m > 0)
            def _():
                dp_copy(m, ft).start()

    def step(t, carry):
        for d in range(2):
            s = t - ((line - 1 - q) if d == 0 else q) * LAG

            @pl.when((s >= 0) & (s < chunks))
            def _():
                process(d, s)

        return carry

    lax.fori_loop(0, chunks + (line - 1) * LAG, step, 0)

    def z_done(s, carry):
        @pl.when(q > 0)
        def _():
            z_copy(0, s).wait_send()

        @pl.when(q < line - 1)
        def _():
            z_copy(1, s).wait_send()

        return carry

    rc = 256
    rtiles = block // rc

    def rel_copy(i, to):
        at = pl.ds(i * rc, rc)
        return pltpu.make_async_remote_copy(
            src_ref=relsend.at[at], dst_ref=relrecv.at[at], send_sem=rs.at[i], recv_sem=rr.at[i],
            device_id=(dp, to), device_id_type=MESH,
        )

    def ending(sd):
        toward = up if sd == 0 else down
        weight = w_ref[0, 0] * inv_len
        sq = jnp.sum(jnp.sum(sqacc[...], axis=1, keepdims=True), axis=0, keepdims=True)
        row = lax.broadcasted_iota(jnp.int32, (8, 128), 0)
        sqbuf[0] = jnp.where(row == 0, jnp.broadcast_to(sq * (weight * weight), (8, 128)), weight)
        sends = [
            pltpu.make_async_remote_copy(
                src_ref=sqbuf.at[0], dst_ref=sqbuf.at[slot], send_sem=ss.at[slot - 1],
                recv_sem=sr.at[slot - 1], device_id=peer, device_id_type=MESH,
            )
            for slot, peer in ends
        ]
        for c in sends:
            c.start()
        lax.fori_loop(0, chunks, z_done, 0)
        for m in range(1, ndp):
            lax.fori_loop(0, ftiles, lambda ft, c, m=m: (dp_copy(m, ft).wait(), c)[1], 0)
        for c in sends:
            c.wait()
        mult = []
        for a in range(ndp):
            base = a * 2 * CORES
            total = sqbuf[base, 0:1, :]
            for i in range(1, 2 * CORES):
                total = total + sqbuf[base + i, 0:1, :]
            factor = jnp.minimum(1.0, bound * lax.rsqrt(total + 1e-06))
            mult.append((factor * sqbuf[base, 1:2, :])[:, 0:1])
        mine = pl.ds(pl.multiple_of(dp * owned, owned), owned)

        def combine(f0):
            cols = slice(f0, f0 + rc)
            value = fin[mine, cols] * mult[0]
            for m in range(1, ndp):
                value = value + dpbuf[m - 1, :, cols] * mult[m]
            return value.T

        far, near = (block, 0) if sd == 0 else (0, block)
        for i in range(rtiles):
            relsend[i * rc : (i + 1) * rc, :] = combine(far + i * rc).astype(relsend.dtype)
            rel_copy(i, toward).start()
        for i in range(rtiles):
            out_ref[i * rc : (i + 1) * rc, :] = combine(near + i * rc)
        for i in range(rtiles):
            rel_copy(i, toward).wait_send()

    @pl.when(q == 0)
    def _():
        ending(0)

    @pl.when(q == line - 1)
    def _():
        ending(1)

    @pl.when(jnp.logical_not(is_end))
    def _():
        lax.fori_loop(0, chunks, z_done, 0)
        for i in range(rtiles):
            rel_copy(i, down).wait_recv()
            out_ref[i * rc : (i + 1) * rc, :] = relrecv[i * rc : (i + 1) * rc, :].astype(jnp.float32)


def fused(hidden, norm_gain, cotangent, loss_weight):
    _, tokens, features = hidden.shape
    outs = cotangent.shape[2]
    ctx = lax.axis_size("ctx")
    ndp = lax.axis_size("dp")
    line = ctx // CORES
    block = features // ctx
    half = features // CORES // 2
    owned = outs // ndp
    fc, rows, groups, pieces = 256, 16, 8, 4
    ftiles = half // fc
    chunks = ftiles * ndp
    cfg = (tokens, features, outs, line, ndp, fc, rows,
           1.0 / math.sqrt(tokens * ctx), math.sqrt(features * outs))
    bf16, f32 = jnp.bfloat16, jnp.float32
    dma = pltpu.SemaphoreType.DMA
    vmem = pl.BlockSpec(memory_space=pltpu.VMEM)
    return pl.pallas_call(
        functools.partial(kernel, cfg),
        name="clipped_grad",
        out_shape=jax.ShapeDtypeStruct((block, owned), f32),
        in_specs=[pl.BlockSpec(memory_space=pl.ANY), vmem, vmem,
                  pl.BlockSpec(memory_space=pltpu.SMEM)],
        out_specs=vmem,
        scratch_shapes=[
            pltpu.VMEM((tokens, features), bf16),
            pltpu.VMEM((tokens, features // CORES), bf16),
            pltpu.VMEM((CORES, outs, tokens), bf16),
            pltpu.VMEM((CORES, tokens, 128), f32),
            pltpu.VMEM((2, CORES * tokens, fc), bf16),
            pltpu.VMEM((2, outs, fc), f32),
            pltpu.VMEM((2, chunks, owned, fc), bf16),
            pltpu.VMEM((2, chunks, owned, fc), bf16),
            pltpu.VMEM((outs, half), f32),
            pltpu.VMEM((ndp - 1, owned, half), f32),
            pltpu.VMEM((8, fc), f32),
            pltpu.VMEM((ndp * 2 * CORES, 8, 128), f32),
            pltpu.VMEM((block, owned), bf16),
            pltpu.VMEM((block, owned), bf16),
            dma((groups,)),
            dma((2 * pieces,)), dma((2 * pieces,)),
            dma((2,)), dma((2,)),
            dma((2, chunks)), dma((2, chunks)),
            dma((ndp - 1, ftiles)), dma((ndp - 1, ftiles)),
            dma((ndp * 2 * CORES - 1,)), dma((ndp * 2 * CORES - 1,)),
            dma((block // 256,)), dma((block // 256,)),
        ],
        compiler_params=pltpu.CompilerParams(
            collective_id=0, has_side_effects=True, vmem_limit_bytes=60 << 20
        ),
    )(hidden[0], norm_gain[None, :], cotangent[0], loss_weight[None, :])


def solution(mesh):
    in_specs = (P("dp", "ctx", None), P(), P("dp", "ctx", None), P("dp"))
    out_specs = P("ctx", "dp")
    short = mesh.shape["ctx"] == 4 * CORES and mesh.shape["dp"] == 4
    body = fused if short else per_device
    return jax.shard_map(body, mesh=mesh, in_specs=in_specs, out_specs=out_specs, check_vma=False)
```

time: 98.2 us -> 88 us (0.90)
  the two profiles are of different devices: /device:TPU:20 before, /device:TPU:0 now
where the time goes in v2:
time: 88 us; the launch traced here: 87.9 us
  Pallas kernels  85.3 us (97%)
  local copies, waits for them, and re-layouts  1.87 us (2%)
    pallas_call x1, Pallas kernels, fused(): pl.pallas_call(functools.partial(kernel, cfg), name='clipped_grad', out_s...  85.3 us
    unnamed x1, local copies, waits for them, and re-layouts  1.87 us

profile of v2, /device:TPU:0, one launch (start us, length us, event | category | flops | bytes accessed | tf_op | source)
XLA Modules:
  0.0 87.9 jit_solution(5179992865674293394)
XLA Ops:
  0.7 85.3 %clipped_grad.1 = f32[1024,128]{1,0:T(8,128)} custom-call(bf16[512,8192]{1,0:T(8,128)(2,1)} %bitcast.5, f32[1,8192]{1,0:T(1,128)} %bitcast.7, bf16[512,512]{1,0:T(8,128)(2,1)} %bitcast.6, f32[1,1]{1,0:T(1,128)} %bitcast.4.w_ref), custom_call_target="tpu_custom_call" | custom-call | tf_op jit(solution)/shard_map/clipped_grad/pallas_call | solution.py:374
  86.0 1.9 %copy.7 = f32[1024,128]{1,0:T(8,128)} copy(f32[1024,128]{1,0:T(8,128)} %clipped_grad.1) | data formatting | bytes 1048576

commit v3 on v2

--- a/solution.py
+++ b/solution.py
@@ -10,7 +10,9 @@
 
 MESH = pl.DeviceIdType.MESH
 CORES = 2
-LAG = 4
+LAG = 3
+SPLIT = 1
+AHEAD = 2
 
 
 def per_device(hidden, norm_gain, cotangent, loss_weight):
@@ -61,8 +63,10 @@
     dpbuf,
     sqacc,
     sqbuf,
-    relsend,
-    relrecv,
+    wide_s,
+    wide_r,
+    slim_s,
+    slim_r,
     ls,
     xs,
     xr,
@@ -82,11 +86,10 @@
     half = features // CORES // 2
     ftiles = half // fc
     owned = outs // ndp
-    chunks = ftiles * ndp
+    chunks = ftiles * ndp * SPLIT
+    part = owned // SPLIT
     groups = ls.shape[0]
     grows = tokens // groups
-    pieces = xs.shape[0] // 2
-    pw = half // pieces
     dp = lax.axis_index("dp")
     ctx = lax.axis_index("ctx")
     q = ctx // CORES
@@ -142,9 +145,10 @@
         return (CORES * (d * (line // 2) + local // block) + core) * block + local % block
 
     def piece_copy(d, p):
-        src = pl.ds(pl.multiple_of(place(d, p * pw, 1 - k), pw), pw)
+        src = pl.ds(pl.multiple_of(place(d, p * fc, 1 - k), fc), fc)
+        dst = pl.ds(pl.multiple_of(d * half + p * fc, fc), fc)
         return pltpu.make_async_remote_copy(
-            src_ref=hid_ref.at[:, src], dst_ref=pr.at[:, pl.ds(d * half + p * pw, pw)],
+            src_ref=hid_ref.at[:, src], dst_ref=pr.at[:, dst],
             send_sem=xs.at[2 * p + d], recv_sem=xr.at[2 * p + d],
             device_id=(dp, other), device_id_type=MESH,
         )
@@ -155,7 +159,7 @@
             device_id=(dp, other), device_id_type=MESH,
         )
 
-    for p in range(pieces):
+    for p in range(AHEAD):
         for d in range(2):
             piece_copy(d, p).start()
         if p == 0:
@@ -200,12 +204,11 @@
         )
 
     def multiply(d, ft):
-        for p in range(pieces):
-
-            @pl.when(ft * fc == p * pw)
-            def _():
-                piece_copy(d, p).wait()
-
+        @pl.when(ft + AHEAD < ftiles)
+        def _():
+            piece_copy(d, ft + AHEAD).start()
+
+        piece_copy(d, ft).wait()
         own = pl.multiple_of(place(d, ft * fc, k), fc)
         got = pl.multiple_of(d * half + ft * fc, fc)
 
@@ -226,14 +229,15 @@
         ) + jnp.dot(ct[1], nt[d, tokens:, :], preferred_element_type=jnp.float32)
 
     def process(d, s):
-        ft = s // ndp
-        m = ndp - 1 - s % ndp
+        ft = s // (ndp * SPLIT)
+        m = ndp - 1 - s // SPLIT % ndp
+        u = s % SPLIT
         h = flip(dp, m)
-        orow = pl.ds(pl.multiple_of(h * owned, owned), owned)
+        orow = pl.ds(pl.multiple_of(h * owned + u * part, part), part)
         first = q == (line - 1 if d == 0 else 0)
         last = q == (0 if d == 0 else line - 1)
 
-        @pl.when(m == ndp - 1)
+        @pl.when((m == ndp - 1) & (u == 0))
         def _():
             multiply(d, ft)
 
@@ -253,9 +257,9 @@
             z_copy(d, s).wait_recv()
             tile = acc[d, orow, :] + rbuf[d, s].astype(jnp.float32)
             fin[orow, pl.ds(pl.multiple_of(ft * fc, fc), fc)] = tile
-            sqacc[...] += jnp.sum((tile * tile).reshape(owned // 8, 8, fc), axis=0)
-
-            @pl.when(m > 0)
+            sqacc[...] += jnp.sum((tile * tile).reshape(part // 8, 8, fc), axis=0)
+
+            @pl.when((m > 0) & (u == SPLIT - 1))
             def _():
                 dp_copy(m, ft).start()
 
@@ -285,10 +289,15 @@
     rc = 256
     rtiles = block // rc
 
+    def relay(i):
+        if i < rtiles // 2:
+            return wide_s, wide_r, pl.ds(i * rc, rc)
+        return slim_s, slim_r, pl.ds((i - rtiles // 2) * rc, rc)
+
     def rel_copy(i, to):
-        at = pl.ds(i * rc, rc)
+        src, dst, at = relay(i)
         return pltpu.make_async_remote_copy(
-            src_ref=relsend.at[at], dst_ref=relrecv.at[at], send_sem=rs.at[i], recv_sem=rr.at[i],
+            src_ref=src.at[at], dst_ref=dst.at[at], send_sem=rs.at[i], recv_sem=rr.at[i],
             device_id=(dp, to), device_id_type=MESH,
         )
 
@@ -331,7 +340,8 @@
 
         far, near = (block, 0) if sd == 0 else (0, block)
         for i in range(rtiles):
-            relsend[i * rc : (i + 1) * rc, :] = combine(far + i * rc).astype(relsend.dtype)
+            src, _, at = relay(i)
+            src[at, :] = combine(far + i * rc).astype(src.dtype)
             rel_copy(i, toward).start()
         for i in range(rtiles):
             out_ref[i * rc : (i + 1) * rc, :] = combine(near + i * rc)
@@ -351,7 +361,8 @@
         lax.fori_loop(0, chunks, z_done, 0)
         for i in range(rtiles):
             rel_copy(i, down).wait_recv()
-            out_ref[i * rc : (i + 1) * rc, :] = relrecv[i * rc : (i + 1) * rc, :].astype(jnp.float32)
+            _, got, at = relay(i)
+            out_ref[i * rc : (i + 1) * rc, :] = got[at, :].astype(jnp.float32)
 
 
 def fused(hidden, norm_gain, cotangent, loss_weight):
@@ -363,9 +374,9 @@
     block = features // ctx
     half = features // CORES // 2
     owned = outs // ndp
-    fc, rows, groups, pieces = 256, 16, 8, 4
+    fc, rows, groups = 256, 16, 8
     ftiles = half // fc
-    chunks = ftiles * ndp
+    chunks = ftiles * ndp * SPLIT
     cfg = (tokens, features, outs, line, ndp, fc, rows,
            1.0 / math.sqrt(tokens * ctx), math.sqrt(features * outs))
     bf16, f32 = jnp.bfloat16, jnp.float32
@@ -385,16 +396,18 @@
             pltpu.VMEM((CORES, tokens, 128), f32),
             pltpu.VMEM((2, CORES * tokens, fc), bf16),
             pltpu.VMEM((2, outs, fc), f32),
-            pltpu.VMEM((2, chunks, owned, fc), bf16),
-            pltpu.VMEM((2, chunks, owned, fc), bf16),
+            pltpu.VMEM((2, chunks, owned // SPLIT, fc), bf16),
+            pltpu.VMEM((2, chunks, owned // SPLIT, fc), bf16),
             pltpu.VMEM((outs, half), f32),
             pltpu.VMEM((ndp - 1, owned, half), f32),
             pltpu.VMEM((8, fc), f32),
             pltpu.VMEM((ndp * 2 * CORES, 8, 128), f32),
-            pltpu.VMEM((block, owned), bf16),
-            pltpu.VMEM((block, owned), bf16),
+            pltpu.VMEM((block // 2, owned), f32),
+            pltpu.VMEM((block // 2, owned), f32),
+            pltpu.VMEM((block // 2, owned), bf16),
+            pltpu.VMEM((block // 2, owned), bf16),
             dma((groups,)),
-            dma((2 * pieces,)), dma((2 * pieces,)),
+            dma((2 * ftiles,)), dma((2 * ftiles,)),
             dma((2,)), dma((2,)),
             dma((2, chunks)), dma((2, chunks)),
             dma((ndp - 1, ftiles)), dma((ndp - 1, ftiles)),

time: 88 us -> 87.5 us (level)
  no operation moved by 1% of the time
where the time goes in v3:
time: 87.5 us; the launch traced here: 87.3 us
  Pallas kernels  84.8 us (97%)
  local copies, waits for them, and re-layouts  1.87 us (2%)
    pallas_call x1, Pallas kernels, fused(): pl.pallas_call(functools.partial(kernel, cfg), name='clipped_grad', out_s...  84.8 us
    unnamed x1, local copies, waits for them, and re-layouts  1.87 us

profile of v3, /device:TPU:0, one launch (start us, length us, event | category | flops | bytes accessed | tf_op | source)
XLA Modules:
  0.0 87.3 jit_solution(1905211615767271382)
XLA Ops:
  0.7 84.8 %clipped_grad.1 = f32[1024,128]{1,0:T(8,128)} custom-call(bf16[512,8192]{1,0:T(8,128)(2,1)} %bitcast.5, f32[1,8192]{1,0:T(1,128)} %bitcast.7, bf16[512,512]{1,0:T(8,128)(2,1)} %bitcast.6, f32[1,1]{1,0:T(1,128)} %bitcast.4.w_ref), custom_call_target="tpu_custom_call" | custom-call | tf_op jit(solution)/shard_map/clipped_grad/pallas_call | solution.py:385
  85.4 1.9 %copy.7 = f32[1024,128]{1,0:T(8,128)} copy(f32[1024,128]{1,0:T(8,128)} %clipped_grad.1) | data formatting | bytes 1048576
